TPU v7x, 32 devices: a whole 2x2x4 slice. The times are simulated.
32 devices in a mesh: span: 8 (over z, x), wall: 4 (over y, core).
Axes of the slice: x: 2, y: 2, z: 4, core: 2. Of those that a mesh axis runs over, the one named last changes fastest.
Arguments:
- velocity: float32 [3, 2, 128, 2048], P(None, None, 'wall', 'span'), may hold values from -6 to 6
- metric: float32 [128], P('wall'), may hold values from 0.5 to 2
Outputs:
- conv: float32 [3, 2, 128, 2048], P(None, None, 'wall', 'span')
- flux: float32 [3, 2, 128, 2048], P(None, None, 'wall', 'span')
All inputs are finite; a program needn't handle non-finite values.
Results may differ from a plain program's by a relative error of at most 0.00014.
Values sent between devices are 32-bit elements; how exact they have to be, the bound alone decides.
A program may use at most 64 MiB of HBM per device.

v0:
```python
import functools
import math

import jax
import jax.numpy as jnp
import numpy as np
from jax import lax
from jax.experimental import pallas as pl
from jax.experimental.pallas import tpu as pltpu
from jax.sharding import PartitionSpec as P

MESH = pl.DeviceIdType.MESH


def split_bf16(table):
    high = table.astype(jnp.bfloat16)
    low = (table - np.asarray(high, np.float64)).astype(jnp.bfloat16)
    return high, low


def make_tables(count, local_len):
    total = count * local_len
    halves = count // 2 + 1
    k1 = np.arange(halves, dtype=np.int64)[:, None]
    m = np.arange(local_len, dtype=np.int64)[None, :]
    angle = 2.0 * math.pi / total * (k1 * m % total)
    wave = k1 + count * m
    signed = np.where(wave < total // 2, wave, wave - total)
    weight = np.where((k1 == 0) | (2 * k1 == count), 1.0, 2.0) / total
    keep = (3 * np.abs(signed) < total) * weight
    kappa = 2.0 * math.pi / total * signed * keep
    small = np.stack([np.cos(angle), -np.sin(angle), keep, kappa]).astype(np.float32)
    small = np.pad(small, ((0, 0), (0, -halves % 8), (0, 0)))
    phase = 2.0 * math.pi / local_len * (m.T * m % local_len)
    table = np.concatenate([np.cos(phase), -np.sin(phase)], axis=1)
    return small, np.stack(split_bf16(table))


def weighted(coeffs, values):
    acc = None
    for coeff, value in zip(coeffs, values):
        if abs(coeff) < 1e-12:
            continue
        if abs(abs(coeff) - 1.0) < 1e-12:
            if acc is None:
                acc = value if coeff > 0 else -value
            else:
                acc = acc + value if coeff > 0 else acc - value
        else:
            term = value * np.float32(coeff)
            acc = term if acc is None else acc + term
    return acc


def real_dft(values):
    n = len(values)
    if n == 1:
        return [(values[0], None)]
    half = n // 2
    sums = [values[p] + values[p + half] for p in range(half)]
    diffs = [values[p] - values[p + half] for p in range(half)]
    bins = [None] * (half + 1)
    for index, item in enumerate(real_dft(sums)):
        bins[2 * index] = item
    for k in range(1, half + 1, 2):
        cosines = [math.cos(2 * math.pi * p * k / n) for p in range(half)]
        sines = [-math.sin(2 * math.pi * p * k / n) for p in range(half)]
        bins[k] = (weighted(cosines, diffs), weighted(sines, diffs))
    return bins


def real_inverse(bins, n):
    if n == 1:
        return [bins[0][0]]
    if n == 2:
        return [bins[0][0] + bins[1][0], bins[0][0] - bins[1][0]]
    half = n // 2
    even = real_inverse(bins[0::2], half)
    odd = []
    ks = list(range(1, half, 2))
    for p in range(half):
        coeffs = [math.cos(2 * math.pi * p * k / n) for k in ks]
        coeffs += [-math.sin(2 * math.pi * p * k / n) for k in ks]
        odd.append(weighted(coeffs, [bins[k][0] for k in ks] + [bins[k][1] for k in ks]))
    return [even[p] + odd[p] for p in range(half)] + [even[p] - odd[p] for p in range(half)]


def dft_rows(rows, dft):
    high = rows.astype(jnp.bfloat16)
    low = (rows - high.astype(jnp.float32)).astype(jnp.bfloat16)
    dot = functools.partial(jnp.dot, preferred_element_type=jnp.float32)
    return dot(high, dft[0]) + dot(low, dft[0]) + dot(high, dft[1])


def kernel(
    dims, source, velocity_hbm, metric, small, dft_hbm, outs,
    planes, ends, wedge, recv, recv_ends, halo, dft, wave_in, wave, obuf,
    local_sem, send_sem, recv_sem, esend_sem, erecv_sem, hsend_sem, hrecv_sem, mine_sem, osend_sem,
    orecv_sem,
):
    count, walls, xs_len, chunk, local_len = dims
    halves = count // 2 + 1
    per_xs = count // xs_len
    span = lax.axis_index("span")
    wall = lax.axis_index("wall")
    place = lax.rem(span, per_xs)
    has_below, has_above = wall > 0, wall < walls - 1

    def wall_at(step):
        return lax.rem(wall + walls + step, walls)

    order = sorted(range(1, count), key=lambda d: abs(d - count // 2))

    def block(ref, index):
        if chunk % 8:
            return ref.at[index]
        at = pl.multiple_of(lax.rem(index, per_xs) * chunk, chunk)
        return ref.at[:, index // per_xs, pl.ds(at, chunk), :]

    stage = pltpu.make_async_copy(velocity_hbm, planes, local_sem.at[4])
    stage.start()
    own = pltpu.make_async_copy(block(source, span), recv.at[span], local_sem.at[1])
    own.start()
    load = pltpu.make_async_copy(dft_hbm, dft, local_sem.at[0])
    load.start()

    barrier = pltpu.get_barrier_semaphore()
    for d in order:
        pl.semaphore_signal(
            barrier, inc=1, device_id=(lax.rem(span + d, count), wall), device_id_type=MESH
        )

    for there, at, step in ((has_below, 0, -1), (has_above, per_xs - 1, 1)):

        @pl.when(there)
        def _():
            @pl.when(place == at)
            def _():
                for p in range(count):
                    pl.semaphore_signal(
                        barrier, inc=1, device_id=(p, wall_at(step)), device_id_type=MESH
                    )

    stage.wait()
    none = jnp.zeros((1, local_len), jnp.float32)

    def plane(x, at):
        if at < 0 or at >= per_xs * chunk:
            return [none] * 3
        return [planes[comp, x, pl.ds(at, 1), :] for comp in range(3)]

    for x in range(xs_len):
        for j in range(per_xs):
            rows = plane(x, j * chunk - 1) + plane(x, (j + 1) * chunk) + [none] * 2
            ends[x * per_xs + j] = jnp.concatenate(rows, axis=0)
        rows = plane(x, per_xs * chunk - 1) + [none] * 5
        wedge[0, x] = jnp.concatenate(rows, axis=0)
        rows = [none] * 3 + plane(x, 0) + [none] * 2
        wedge[1, x] = jnp.concatenate(rows, axis=0)

    sides = (wall + walls - 1) // walls + (2 * walls - 2 - wall) // walls
    pl.semaphore_wait(barrier, count - 1 + xs_len * sides)

    sends = []
    arrivals = [[] for _ in range(3)]
    for comp in range(3):
        for d in order:
            peer = lax.rem(span + d, count)
            copy = pltpu.make_async_remote_copy(
                src_ref=block(source, peer).at[comp],
                dst_ref=recv.at[span, comp],
                send_sem=send_sem.at[comp, d],
                recv_sem=recv_sem.at[comp, d],
                device_id=(peer, wall),
                device_id_type=MESH,
            )
            copy.start()
            arrivals[comp].append(copy)
    for d in order:
        peer = lax.rem(span + d, count)
        copy = pltpu.make_async_remote_copy(
            src_ref=ends.at[peer],
            dst_ref=recv_ends.at[span],
            send_sem=esend_sem.at[d],
            recv_sem=erecv_sem.at[d],
            device_id=(peer, wall),
            device_id_type=MESH,
        )
        copy.start()
        sends.append(copy)
    own_ends = pltpu.make_async_copy(ends.at[span], recv_ends.at[span], local_sem.at[5])
    own_ends.start()

    def halo_copy(side, x):
        if side == 0:
            target = (x * per_xs, wall_at(1))
        else:
            target = (x * per_xs + per_xs - 1, wall_at(-1))
        return pltpu.make_async_remote_copy(
            src_ref=wedge.at[side, x],
            dst_ref=halo.at[side, span],
            send_sem=hsend_sem.at[side, x],
            recv_sem=hrecv_sem.at[side, span],
            device_id=target,
            device_id_type=MESH,
        )

    def halo_arrival(side, p):
        return pltpu.make_async_remote_copy(
            src_ref=wedge.at[side, 0],
            dst_ref=halo.at[side, p],
            send_sem=hsend_sem.at[side, 0],
            recv_sem=hrecv_sem.at[side, p],
            device_id=(p, wall_at(2 * side - 1)),
            device_id_type=MESH,
        )

    for side, there in ((0, has_above), (1, has_below)):

        @pl.when(there)
        def _():
            for x in range(xs_len):
                halo_copy(side, x).start()

    load.wait()
    own.wait()

    def wait_component(comp):
        for copy in arrivals[comp]:
            copy.wait_recv()

    def wait_edges():
        own_ends.wait()
        for copy in sends:
            copy.wait_recv()
        for side, there, at in ((0, has_below, 0), (1, has_above, per_xs - 1)):

            @pl.when(there)
            def _():
                @pl.when(place == at)
                def _():
                    row = lax.broadcasted_iota(jnp.int32, (8, local_len), 0)
                    taken = row < 3 if side == 0 else row >= 3
                    for p in range(count):
                        halo_arrival(side, p).wait_recv()
                        recv_ends[p] = jnp.where(taken, halo[side, p], recv_ends[p])

    row = lax.broadcasted_iota(jnp.int32, (chunk, local_len), 0)
    scale = jnp.zeros((chunk, local_len), jnp.float32)
    for j in range(chunk):
        scale = jnp.where(row == j, metric[place * chunk + j], scale)

    def velocity(p, comp):
        return recv[p, comp]

    def product(first, second):
        return [velocity(p, first) * velocity(p, second) for p in range(count)]

    def slope(first, second):
        fields = []
        for p in range(count):
            edge = recv_ends[p]
            below = edge[first : first + 1] * edge[second : second + 1]
            above = edge[3 + first : 4 + first] * edge[3 + second : 4 + second]
            inner = velocity(p, first) * velocity(p, second)
            upper = jnp.concatenate([inner[1:], above], axis=0)
            lower = jnp.concatenate([below, inner[:-1]], axis=0)
            fields.append((upper - lower) * scale)
        return fields

    def twiddle(k):
        return small[0, pl.ds(k, 1), :], small[1, pl.ds(k, 1), :]

    def rows_of(ref, start, stop):
        return ref[:, start:stop].reshape(2 * (stop - start) * ref.shape[2], local_len)

    def forward(start, fields):
        for number, values in enumerate(fields):
            for k, (real, imag) in enumerate(real_dft(values)):
                at = (start + number) * halves + k
                tw_cos, tw_sin = twiddle(k)
                if imag is None:
                    wave_in[0, at, 0:chunk, :] = real * tw_cos
                    wave_in[1, at, 0:chunk, :] = real * tw_sin
                else:
                    wave_in[0, at, 0:chunk, :] = real * tw_cos - imag * tw_sin
                    wave_in[1, at, 0:chunk, :] = real * tw_sin + imag * tw_cos
        first, last = start * halves, (start + len(fields)) * halves
        both = dft_rows(rows_of(wave_in, first, last), dft)
        both = both.reshape(2, last - first, wave.shape[2], 2 * local_len)
        by_cos, by_sin = both[..., :local_len], both[..., local_len:]
        wave[0, first:last] = by_cos[0] - by_sin[1]
        wave[1, first:last] = by_sin[0] + by_cos[1]

    copies = []

    def deliver(group, number, filtered):
        slot = 3 * group + number
        for k in range(halves):
            real, imag = filtered(number, k)
            wave_in[0, k] = real
            wave_in[1, k] = imag
        both = dft_rows(rows_of(wave_in, 0, halves), dft)
        both = both.reshape(2, halves, wave.shape[2], 2 * local_len)
        by_cos, by_sin = both[..., :local_len], both[..., local_len:]
        bins = []
        for k in range(halves):
            real = by_cos[0, k] + by_sin[1, k]
            imag = by_cos[1, k] - by_sin[0, k]
            tw_cos, tw_sin = twiddle(k)
            bins.append((real * tw_cos + imag * tw_sin, imag * tw_cos - real * tw_sin))
        for p, value in enumerate(real_inverse(bins, count)):
            obuf[slot, p] = value[0:chunk]
        target = block(outs.at[group], span).at[number]
        mine = pltpu.make_async_copy(obuf.at[slot, span], target, mine_sem.at[slot])
        mine.start()
        copies.append(mine)
        for d in order:
            peer = lax.rem(span + d, count)
            copy = pltpu.make_async_remote_copy(
                src_ref=obuf.at[slot, peer],
                dst_ref=target,
                send_sem=osend_sem.at[slot, d],
                recv_sem=orecv_sem.at[slot, d],
                device_id=(peer, wall),
                device_id_type=MESH,
            )
            copy.start()
            copies.append(copy)

    def keep_only(number, k):
        keep = small[2, pl.ds(k, 1), :]
        at = number * halves + k
        return wave[0, at] * keep, wave[1, at] * keep

    def divergence(number, k):
        keep, kappa = small[2, pl.ds(k, 1), :], small[3, pl.ds(k, 1), :]
        at_y = ((3, 4, 6)[number]) * halves + k
        at_z = ((2, 5, 7)[number]) * halves + k
        real = wave[0, at_y] * keep - wave[1, at_z] * kappa
        imag = wave[1, at_y] * keep + wave[0, at_z] * kappa
        return real, imag

    for comp in range(3):
        wait_component(comp)
        forward(comp, [product(0, comp)])
        deliver(0, comp, keep_only)
    wait_edges()
    forward(3, [slope(0, 1)])
    deliver(1, 0, divergence)
    forward(4, [slope(1, 1), product(1, 2)])
    deliver(1, 1, divergence)
    forward(6, [slope(1, 2), product(2, 2)])
    deliver(1, 2, divergence)

    for copy in sum(arrivals, sends):
        copy.wait_send()
    for side, there in ((0, has_above), (1, has_below)):

        @pl.when(there)
        def _():
            for x in range(xs_len):
                halo_copy(side, x).wait_send()

    for copy in copies:
        copy.wait()


def body(walls, velocity, metric):
    count = lax.axis_size("span")
    _, xs_len, yl_len, local_len = velocity.shape
    per_xs = count // xs_len
    chunk = yl_len // per_xs
    halves = count // 2 + 1
    rows = 8 * ((chunk + 7) // 8)
    small, dft = make_tables(count, local_len)

    blocks = (count, 3, chunk, local_len)
    out_shape = velocity.shape
    source = velocity
    if chunk % 8:
        source = velocity.reshape(3, xs_len, per_xs, chunk, local_len)
        source = source.transpose(1, 2, 0, 3, 4).reshape(blocks)
        out_shape = blocks

    in_vmem = pl.BlockSpec(memory_space=pltpu.VMEM)
    in_smem = pl.BlockSpec(memory_space=pltpu.SMEM)
    anywhere = pl.BlockSpec(memory_space=pl.ANY)
    dma = pltpu.SemaphoreType.DMA
    f32 = jnp.float32
    outs = pl.pallas_call(
        functools.partial(kernel, (count, walls, xs_len, chunk, local_len)),
        out_shape=jax.ShapeDtypeStruct((2,) + out_shape, f32),
        in_specs=[anywhere, anywhere, in_smem, in_vmem, anywhere],
        out_specs=anywhere,
        scratch_shapes=[
            pltpu.VMEM(velocity.shape, f32),
            pltpu.VMEM((count, 8, local_len), f32),
            pltpu.VMEM((2, xs_len, 8, local_len), f32),
            pltpu.VMEM(blocks, f32),
            pltpu.VMEM((count, 8, local_len), f32),
            pltpu.VMEM((2, count, 8, local_len), f32),
            pltpu.VMEM(dft.shape, jnp.bfloat16),
            pltpu.VMEM((2, 8 * halves, rows, local_len), f32),
            pltpu.VMEM((2, 8 * halves, rows, local_len), f32),
            pltpu.VMEM((6, count, chunk, local_len), f32),
            dma((6,)),
            dma((3, count)),
            dma((3, count)),
            dma((count,)),
            dma((count,)),
            dma((2, xs_len)),
            dma((2, count)),
            dma((6,)),
            dma((6, count)),
            dma((6, count)),
        ],
        compiler_params=pltpu.CompilerParams(collective_id=0, has_side_effects=True),
        name="convect",
    )(source, velocity, metric, jnp.asarray(small), jnp.asarray(dft))
    flux, conv = outs[0], outs[1]
    if chunk % 8:
        planes = [
            out.reshape(xs_len, per_xs, 3, chunk, local_len).transpose(2, 0, 1, 3, 4)
            for out in (flux, conv)
        ]
        flux, conv = [out.reshape(velocity.shape) for out in planes]
    return (conv, flux)


def solution(mesh):
    spec = P(None, None, "wall", "span")
    return jax.shard_map(
        functools.partial(body, mesh.shape["wall"]),
        mesh=mesh,
        in_specs=(spec, P("wall")),
        out_specs=(spec, spec),
        check_vma=False,
    )
```

profile of v0, /device:TPU:0, one launch (start us, length us, event | category | flops | bytes accessed | tf_op | source)
XLA Modules:
  0.0 28.5 jit_solution(10553691663664716072)
XLA Ops:
  0.6 26.1 %convect.1 = f32[2,3,2,32,256]{4,3,2,1,0:T(8,128)} custom-call(f32[3,2,32,256]{3,2,1,0:T(8,128)} %velocity_hbm.1, f32[3,2,32,256]{3,2,1,0:T(8,128)} %velocity_hbm.1, f32[32]{0:T(128)} %metric.1, f32[4,8,256]{2,1,0:T(8,128)} %constant.4.clone.small, bf16[2,256,512]{2,1,0:T(8,128)(2,1)} %constant.5.clone.dft_hbm), custom_call_target="tpu_custom_call" | custom-call | tf_op jit(solution)/shard_map/convect/pallas_call | solution.py:391
  26.7 1.8 %slice_bitcast_fusion = (f32[3,2,32,256]{3,2,1,0:T(8,128)}, f32[3,2,32,256]{3,2,1,0:T(8,128)}) fusion(f32[2,3,2,32,256]{4,3,2,1,0:T(8,128)} %convect.1), kind=kLoop, calls=%fused_computation | loop fusion | bytes 786432 | tf_op jit(solution)/shard_map/squeeze | solution.py:421
where the time goes:
time: 28.8 us; the launch traced here: 28.5 us
  Pallas kernels  26.1 us (91%)
  local copies, waits for them, and re-layouts  1.79 us (6%)
  between operations  0.64 us (2%)
    pallas_call x1, Pallas kernels, body(): pl.pallas_call(functools.partial(kernel, (count, walls, xs_len, chunk, lo...  26.1 us
    squeeze x1, local copies, waits for them, and re-layouts, body(): flux, conv = (outs[0], outs[1])  1.79 us

commit v1 on v0

--- a/solution.py
+++ b/solution.py
@@ -93,8 +93,8 @@
 
 
 def kernel(
-    dims, source, velocity_hbm, metric, small, dft_hbm, outs,
-    planes, ends, wedge, recv, recv_ends, halo, dft, wave_in, wave, obuf,
+    dims, source, velocity_hbm, metric_hbm, small_hbm, dft_hbm, flux, conv,
+    metric, small, planes, ends, wedge, recv, recv_ends, halo, dft, wave_in, wave, obuf,
     local_sem, send_sem, recv_sem, esend_sem, erecv_sem, hsend_sem, hrecv_sem, mine_sem, osend_sem,
     orecv_sem,
 ):
@@ -117,13 +117,6 @@
         at = pl.multiple_of(lax.rem(index, per_xs) * chunk, chunk)
         return ref.at[:, index // per_xs, pl.ds(at, chunk), :]
 
-    stage = pltpu.make_async_copy(velocity_hbm, planes, local_sem.at[4])
-    stage.start()
-    own = pltpu.make_async_copy(block(source, span), recv.at[span], local_sem.at[1])
-    own.start()
-    load = pltpu.make_async_copy(dft_hbm, dft, local_sem.at[0])
-    load.start()
-
     barrier = pltpu.get_barrier_semaphore()
     for d in order:
         pl.semaphore_signal(
@@ -140,6 +133,17 @@
                     pl.semaphore_signal(
                         barrier, inc=1, device_id=(p, wall_at(step)), device_id_type=MESH
                     )
+
+    stage = pltpu.make_async_copy(velocity_hbm, planes, local_sem.at[4])
+    stage.start()
+    own = pltpu.make_async_copy(block(source, span), recv.at[span], local_sem.at[1])
+    own.start()
+    load = pltpu.make_async_copy(dft_hbm, dft, local_sem.at[0])
+    load.start()
+    tables = pltpu.make_async_copy(small_hbm, small, local_sem.at[2])
+    tables.start()
+    scales = pltpu.make_async_copy(metric_hbm, metric, local_sem.at[3])
+    scales.start()
 
     stage.wait()
     none = jnp.zeros((1, local_len), jnp.float32)
@@ -224,6 +228,8 @@
 
     load.wait()
     own.wait()
+    tables.wait()
+    scales.wait()
 
     def wait_component(comp):
         for copy in arrivals[comp]:
@@ -311,7 +317,7 @@
             bins.append((real * tw_cos + imag * tw_sin, imag * tw_cos - real * tw_sin))
         for p, value in enumerate(real_inverse(bins, count)):
             obuf[slot, p] = value[0:chunk]
-        target = block(outs.at[group], span).at[number]
+        target = block((flux, conv)[group], span).at[number]
         mine = pltpu.make_async_copy(obuf.at[slot, span], target, mine_sem.at[slot])
         mine.start()
         copies.append(mine)
@@ -366,6 +372,17 @@
         copy.wait()
 
 
+def store(flux_in, conv_in, flux, conv, sem):
+    copies = [
+        pltpu.make_async_copy(flux_in, flux, sem.at[0]),
+        pltpu.make_async_copy(conv_in, conv, sem.at[1]),
+    ]
+    for copy in copies:
+        copy.start()
+    for copy in copies:
+        copy.wait()
+
+
 def body(walls, velocity, metric):
     count = lax.axis_size("span")
     _, xs_len, yl_len, local_len = velocity.shape
@@ -383,17 +400,18 @@
         source = source.transpose(1, 2, 0, 3, 4).reshape(blocks)
         out_shape = blocks
 
-    in_vmem = pl.BlockSpec(memory_space=pltpu.VMEM)
-    in_smem = pl.BlockSpec(memory_space=pltpu.SMEM)
     anywhere = pl.BlockSpec(memory_space=pl.ANY)
     dma = pltpu.SemaphoreType.DMA
     f32 = jnp.float32
-    outs = pl.pallas_call(
+    operands = (source, velocity, metric, jnp.asarray(small), jnp.asarray(dft))
+    flux, conv = pl.pallas_call(
         functools.partial(kernel, (count, walls, xs_len, chunk, local_len)),
-        out_shape=jax.ShapeDtypeStruct((2,) + out_shape, f32),
-        in_specs=[anywhere, anywhere, in_smem, in_vmem, anywhere],
-        out_specs=anywhere,
+        out_shape=[pltpu.VMEM(out_shape, f32)] * 2,
+        in_specs=[anywhere] * 5,
+        out_specs=[anywhere] * 2,
         scratch_shapes=[
+            pltpu.SMEM(metric.shape, f32),
+            pltpu.VMEM(small.shape, f32),
             pltpu.VMEM(velocity.shape, f32),
             pltpu.VMEM((count, 8, local_len), f32),
             pltpu.VMEM((2, xs_len, 8, local_len), f32),
@@ -415,10 +433,20 @@
             dma((6, count)),
             dma((6, count)),
         ],
-        compiler_params=pltpu.CompilerParams(collective_id=0, has_side_effects=True),
+        compiler_params=pltpu.CompilerParams(
+            collective_id=0, has_side_effects=True, vmem_limit_bytes=32 * 2**20
+        ),
         name="convect",
-    )(source, velocity, metric, jnp.asarray(small), jnp.asarray(dft))
-    flux, conv = outs[0], outs[1]
+    )(*[pltpu.with_memory_space_constraint(x, pltpu.HBM) for x in operands])
+    flux, conv = pl.pallas_call(
+        store,
+        out_shape=[pltpu.HBM(out_shape, f32)] * 2,
+        in_specs=[anywhere] * 2,
+        out_specs=[anywhere] * 2,
+        scratch_shapes=[dma((2,))],
+        compiler_params=pltpu.CompilerParams(vmem_limit_bytes=2**20),
+        name="store",
+    )(flux, conv)
     if chunk % 8:
         planes = [
             out.reshape(xs_len, per_xs, 3, chunk, local_len).transpose(2, 0, 1, 3, 4)

time: 28.8 us -> 26.9 us (0.934)
  local copies, waits for them, and re-layouts: 1.79 us -> 0 us
    squeeze x1 -> x0, local copies, waits for them, and re-layouts: 1.79 us -> none  [body(): flux, conv = (outs[0], outs[1])]
    pallas_call x0 -> x1, Pallas kernels: none -> 0.76 us  [body(): pl.pallas_call(store, out_shape=[pltpu.HBM(out_shape, f32)] * 2, in_specs...]
    pallas_call x1, Pallas kernels: 26.1 us -> 25.4 us  [body(): pl.pallas_call(functools.partial(kernel, (count, walls, xs_len, chunk, lo...]
where the time goes in v1:
time: 26.9 us; the launch traced here: 26.8 us
  Pallas kernels  26.1 us (97%)
  between operations  0.64 us (2%)
    pallas_call x1, Pallas kernels, body(): pl.pallas_call(functools.partial(kernel, (count, walls, xs_len, chunk, lo...  25.4 us
    pallas_call x1, Pallas kernels, body(): pl.pallas_call(store, out_shape=[pltpu.HBM(out_shape, f32)] * 2, in_specs...  0.76 us

profile of v1, /device:TPU:0, one launch (start us, length us, event | category | flops | bytes accessed | tf_op | source)
XLA Modules:
  0.0 26.8 jit_solution(18098439444403533305)
XLA Ops:
  0.6 25.4 %convect.1 = (f32[3,2,32,256]{3,2,1,0:T(8,128)S(1)}, f32[3,2,32,256]{3,2,1,0:T(8,128)S(1)}) custom-call(f32[3,2,32,256]{3,2,1,0:T(8,128)} %velocity_hbm.1, f32[3,2,32,256]{3,2,1,0:T(8,128)} %velocity_hbm.1, f32[32]{0:T(128)} %metric_hbm.1, f32[4,8,256]{2,1,0:T(8,128)} %constant.4.clone.small_hbm, bf16[2,256,512]{2,1,0:T(8,128)(2,1)} %constant.5.clone.dft_hbm), custom_call_target="tpu_custom_call" | custom-call | tf_op jit(solution)/shard_map/convect/pallas_call | solution.py:407
  26.0 0.8 %store.1 = (f32[3,2,32,256]{3,2,1,0:T(8,128)}, f32[3,2,32,256]{3,2,1,0:T(8,128)}) custom-call(f32[3,2,32,256]{3,2,1,0:T(8,128)S(1)} %get-tuple-element.6.flux_in, f32[3,2,32,256]{3,2,1,0:T(8,128)S(1)} %get-tuple-element.7.conv_in), custom_call_target="tpu_custom_call" | custom-call | tf_op jit(solution)/shard_map/store/pallas_call | solution.py:441

commit v2 on v1

--- a/solution.py
+++ b/solution.py
@@ -183,8 +183,8 @@
     for d in order:
         peer = lax.rem(span + d, count)
         copy = pltpu.make_async_remote_copy(
-            src_ref=ends.at[peer],
-            dst_ref=recv_ends.at[span],
+            src_ref=ends.at[peer, pl.ds(0, 6)],
+            dst_ref=recv_ends.at[span, pl.ds(0, 6)],
             send_sem=esend_sem.at[d],
             recv_sem=erecv_sem.at[d],
             device_id=(peer, wall),

time: 26.9 us -> 26.4 us (0.981)
  Pallas kernels: 26.1 us -> 25.6 us
    pallas_call x1, Pallas kernels: 25.4 us -> 24.9 us  [body(): pl.pallas_call(functools.partial(kernel, (count, walls, xs_len, chunk, lo...]
where the time goes in v2:
time: 26.4 us; the launch traced here: 26.3 us
  Pallas kernels  25.6 us (97%)
  between operations  0.64 us (2%)
    pallas_call x1, Pallas kernels, body(): pl.pallas_call(functools.partial(kernel, (count, walls, xs_len, chunk, lo...  24.9 us
    pallas_call x1, Pallas kernels, body(): pl.pallas_call(store, out_shape=[pltpu.HBM(out_shape, f32)] * 2, in_specs...  0.76 us

profile of v2, /device:TPU:0, one launch (start us, length us, event | category | flops | bytes accessed | tf_op | source)
XLA Modules:
  0.0 26.3 jit_solution(10636221837146603664)
XLA Ops:
  0.6 24.9 %convect.1 = (f32[3,2,32,256]{3,2,1,0:T(8,128)S(1)}, f32[3,2,32,256]{3,2,1,0:T(8,128)S(1)}) custom-call(f32[3,2,32,256]{3,2,1,0:T(8,128)} %velocity_hbm.1, f32[3,2,32,256]{3,2,1,0:T(8,128)} %velocity_hbm.1, f32[32]{0:T(128)} %metric_hbm.1, f32[4,8,256]{2,1,0:T(8,128)} %constant.4.clone.small_hbm, bf16[2,256,512]{2,1,0:T(8,128)(2,1)} %constant.5.clone.dft_hbm), custom_call_target="tpu_custom_call" | custom-call | tf_op jit(solution)/shard_map/convect/pallas_call | solution.py:407
  25.5 0.8 %store.1 = (f32[3,2,32,256]{3,2,1,0:T(8,128)}, f32[3,2,32,256]{3,2,1,0:T(8,128)}) custom-call(f32[3,2,32,256]{3,2,1,0:T(8,128)S(1)} %get-tuple-element.6.flux_in, f32[3,2,32,256]{3,2,1,0:T(8,128)S(1)} %get-tuple-element.7.conv_in), custom_call_target="tpu_custom_call" | custom-call | tf_op jit(solution)/shard_map/store/pallas_call | solution.py:441
